TPU v7x, 512 devices: a whole 4x4x16 slice. The times are simulated.
512 devices in a mesh: fsdp: 16 (over x, y_lo, core), tm: 32 (over y_hi, z).
Axes of the slice: x: 4, y: 4 (y_hi: 2, y_lo: 2; y = y_hi * 2 + y_lo), z: 16, core: 2. Of those that a mesh axis runs over, the one named last changes fastest.
Arguments:
- tokens: bfloat16 [32, 32, 256, 1024], P('fsdp', 'tm'), may hold values from -6 to 6
- spatial_gain: float32 [1024], replicated, may hold values from 0.25 to 1.75
- spatial_qkv: bfloat16 [1024, 1536], P('fsdp'), may hold values from -16 to 16
- spatial_out: bfloat16 [512, 1024], P('fsdp'), may hold values from -0.25 to 0.25
- temporal_gain: float32 [1024], replicated, may hold values from 0.25 to 1.75
- temporal_qkv: bfloat16 [1024, 1536], P('fsdp'), may hold values from -16 to 16
- temporal_out: bfloat16 [512, 1024], P('fsdp'), may hold values from -0.25 to 0.25
Outputs:
- encoded: bfloat16 [32, 32, 256, 1024], P('fsdp', 'tm')
All inputs are finite; a program needn't handle non-finite values.
Results may differ from a plain program's by a relative error of at most 0.0061.
Values may be sent and summed in bfloat16 or wider, within the bound.
No kernel may reach another device: no remote copies, remote signals or barrier semaphores. Data moves between devices by JAX's collectives and lax.ppermute only.
A program may use at most 64 MiB of HBM per device.

v0:
```python
import jax
import jax.numpy as jnp
from jax import lax
from jax.sharding import PartitionSpec as P

HEAD = 64
HEADS = 8
INNER = 512
EPSILON = 1e-06


def laid_out(pieces, dim):
    pieces = jnp.moveaxis(pieces, 0, dim)
    shape = pieces.shape
    return pieces.reshape(*shape[:dim], shape[dim] * shape[dim + 1], *shape[dim + 2 :])


def sent_to_all(shard, axis):
    copies = jnp.broadcast_to(shard, (lax.axis_size(axis), *shard.shape))
    return lax.all_to_all(copies, axis, split_axis=0, concat_axis=0, tiled=True)


def gathered_copies(shard, axis, dim):
    return laid_out(sent_to_all(shard, axis), dim)


def norm_rows(source, norm_gain):
    values = source.astype(jnp.float32)
    centre = values - jnp.mean(values, axis=-1, keepdims=True)
    spread = jnp.mean(centre * centre, axis=-1, keepdims=True)
    return (centre * lax.rsqrt(spread + EPSILON) * norm_gain).astype(jnp.bfloat16)


def attention_core(projected):
    inner_width = projected.shape[-1] // 3
    lead_shape = projected.shape[:-1]
    queries = projected[..., :inner_width].reshape(lead_shape + (HEADS, HEAD))
    key_rows = projected[..., inner_width : 2 * inner_width].reshape(lead_shape + (HEADS, HEAD))
    value_rows = (
        projected[..., 2 * inner_width :].astype(jnp.bfloat16).reshape(lead_shape + (HEADS, HEAD))
    )
    scores = jnp.einsum("blmhe,bkmhe->bmhlk", queries, key_rows) * HEAD ** (-0.5)
    row_max = jnp.max(scores, axis=-1, keepdims=True)
    exponent = jnp.exp(scores - row_max)
    weights = (exponent / jnp.sum(exponent, axis=-1, keepdims=True)).astype(jnp.bfloat16)
    context = jnp.einsum(
        "bmhlk,bkmhe->blmhe", weights, value_rows, preferred_element_type=jnp.float32
    )
    return context.astype(jnp.bfloat16).reshape(lead_shape + (inner_width,))


def project_inputs(normed, weight):

    def add_rows(running, segment, offset):
        return jnp.dot(normed, segment, preferred_element_type=jnp.float32)

    initial = jnp.zeros((normed.shape[0], weight.shape[1]), jnp.float32)
    return add_rows(initial, lax.all_gather(weight, "fsdp", axis=0, tiled=True), jnp.int32(0))


def project_outputs(context, weight):

    def add_rows(running, segment, offset):
        return jnp.dot(context, segment, preferred_element_type=jnp.float32)

    initial = jnp.zeros((context.shape[0], weight.shape[1]), jnp.float32)
    return add_rows(initial, gathered_copies(weight, "fsdp", 0), jnp.int32(0))


def shards(
    tokens, spatial_gain, spatial_qkv, spatial_out, temporal_gain, temporal_qkv, temporal_out
):
    clip_count, frames, places, feature_width = tokens.shape
    row_count = clip_count * frames * places
    normed = norm_rows(tokens, spatial_gain).reshape(row_count, feature_width)
    projected = project_inputs(normed, spatial_qkv).reshape(
        clip_count * frames, places, 1, 3 * INNER
    )
    context = attention_core(projected).reshape(row_count, INNER)
    middle = (
        tokens.reshape(row_count, feature_width).astype(jnp.float32)
        + project_outputs(context, spatial_out)
    ).astype(jnp.bfloat16)
    middle = middle.reshape(clip_count, frames, places, feature_width)
    arrived = lax.all_to_all(middle, "tm", split_axis=2, concat_axis=1, tiled=True)
    full_frames = arrived.shape[1]
    few_places = arrived.shape[2]
    normed_t = norm_rows(arrived, temporal_gain).reshape(row_count, feature_width)
    projected_t = project_inputs(normed_t, temporal_qkv).reshape(
        clip_count, full_frames, few_places, 3 * INNER
    )
    context_t = attention_core(projected_t)
    returned_ctx = lax.all_to_all(context_t, "tm", split_axis=1, concat_axis=2, tiled=True)
    finished = middle.reshape(row_count, feature_width).astype(jnp.float32) + project_outputs(
        returned_ctx.reshape(row_count, INNER), temporal_out
    )
    return finished.astype(jnp.bfloat16).reshape(clip_count, frames, places, feature_width)


def solution(mesh):
    placed = (
        P("fsdp", "tm", None, None),
        P(),
        P("fsdp", None),
        P("fsdp", None),
        P(),
        P("fsdp", None),
        P("fsdp", None),
    )
    return jax.shard_map(
        shards, mesh=mesh, in_specs=placed, out_specs=P("fsdp", "tm", None, None), check_vma=False
    )
```

profile of v0, /device:TPU:32, one launch (start us, length us, event | category | flops | bytes accessed | tf_op | source)
XLA Modules:
  0.0 228.6 jit_solution(6030307744431917893)
XLA Ops:
  6.5 0.7 all-gather.3.cloned.1.call-update
  7.3 1.9 broadcast_in_dim.4
  9.2 5.6 %all-to-all-start = ((bf16[16,32,1024]{2,1,0:T(8,128)(2,1)}), bf16[16,32,1024]{2,1,0:T(8,128)(2,1)}, u32[]{:S(2)}, u32[]{:S(2)}) async-start(bf16[16,32,1024]{2,1,0:T(8,128)(2,1)} %broadcast_in_dim.4), calls=%async_computation | async-start | bytes 2097152 | tf_op jit(solution)/shard_map/all_to_all | solution.py:20
  14.9 0.7 all-gather.5.cloned.1.call-update
  15.6 0.2 convert_reduce_fusion
  15.8 0.4 multiply_reduce_fusion.2
  16.2 40.8 %all-gather.3.cloned.1.call-done = bf16[1024,1536]{1,0:T(8,128)(2,1)} async-done(((bf16[64,1536]{1,0:T(8,128)(2,1)}), bf16[1024,1536]{1,0:T(8,128)(2,1)}) %all-gather.3.cloned.1.call-update) | async-done | bytes 3145744 | tf_op jit(solution)/shard_map/all_gather | solution.py:58
  57.0 3.8 %convolution_bitcast_fusion = bf16[2,256,1,1536]{3,1,0,2:T(8,128)(2,1)S(1)} fusion(bf16[1024,1536]{1,0:T(8,128)(2,1)} %all-gather.3.cloned.1.call-done, bf16[2,1,256,1024]{3,2,1,0:T(8,128)(2,1)S(1)} %copy-done, f32[1024]{0:T(1024)S(1)} %copy-done.4, f32[2,256]{1,0:T(2,128)S(1)} %add_rsqrt_fusion.1, f32[2,256]{1,0:T(2,128)S(1)} %broadcast_multiply_fusion.1), kind=kOutput, calls=%fused_computation.6 | convolution fusion | flops 1613234176 | bytes 5775360 | tf_op jit(solution)/shard_map/dot_general | solution.py:55
  61.6 3.5 %fusion.39 = (f32[2,8,256]{2,1,0:T(8,128)S(1)}, f32[2,8,256,256]{2,3,1,0:T(8,128)}) fusion(bf16[2,256,8,64]{1,3,2,0:T(8,128)(2,1)S(1)} %bitcast.67, bf16[2,256,8,64]{1,3,2,0:T(8,128)(2,1)S(1)} %bitcast.69), kind=kOutput, calls=%fused_computation.56 | convolution fusion | flops 137363712 | bytes 5259264 | tf_op jit(solution)/shard_map/sub | solution.py:44
  65.0 2.7 %fusion.20 = bf16[2,256,1,8,64]{1,4,3,0,2:T(8,128)(2,1)S(1)} fusion(bf16[2,256,8,64]{1,3,2,0:T(8,128)(2,1)S(1)} %bitcast.70, f32[2,8,256,256]{2,3,1,0:T(8,128)} %get-tuple-element.12, f32[2,8,256]{2,1,0:T(8,128)S(1)} %get-tuple-element.11), kind=kOutput, calls=%fused_computation.33 | convolution fusion | flops 136577024 | bytes 5259264 | tf_op jit(solution)/shard_map/bmhlk,bkmhe->blmhe/dot_general | solution.py:46
  67.7 0.5 copy.82
  68.4 2.0 fusion.8
  70.3 1.1 copy.83
  71.4 71.4 %all_to_all.28 = bf16[2,1,256,1024]{3,0,1,2:T(2,128)(2,1)S(1)} all-to-all(bf16[2,1,256,1024]{3,0,1,2:T(2,128)(2,1)S(1)} %copy.83), channel_id=1, replica_groups=mesh['fsdp'=16,'tm'=32] {'tm'}, dimensions={2} | all-to-all | bytes 2097152 | tf_op jit(solution)/shard_map/all_to_all | solution.py:85
  142.9 0.9 convert_reduce_fusion.1
  143.8 1.8 multiply_reduce_fusion.1
  145.6 0.3 copy.118
  145.9 0.3 copy.119
  146.2 0.9 convert.12
  147.1 4.0 %fusion.5 = bf16[2,32,8,1536]{3,2,1,0:T(8,128)(2,1)S(1)} fusion(bf16[1024,1536]{1,0:T(8,128)(2,1)} %all-gather.5.cloned.1.call-done, f32[2,32,8,1024]{3,0,2,1:T(2,128)S(1)} %convert.12, f32[1024]{0:T(1024)S(1)} %copy-done.5, f32[2,32,8]{2,1,0:T(8,128)S(1)} %copy.118, f32[2,32,8]{2,1,0:T(8,128)S(1)} %copy.119), kind=kOutput, calls=%fused_computation.7 | convolution fusion | flops 1612709888 | bytes 6823936 | tf_op jit(solution)/shard_map/dot_general | solution.py:55
  151.3 0.5 reshape.163
  151.8 0.5 reshape.164
  152.3 1.5 reshape.162
  153.9 3.2 %fusion.40 = (f32[2,8,8,32]{3,2,1,0:T(8,128)S(1)}, f32[2,8,8,32,32]{3,4,2,1,0:T(8,128)}) fusion(bf16[2,32,8,8,64]{4,3,2,1,0:T(8,128)(2,1)S(1)} %reshape.164, bf16[2,32,8,8,64]{4,3,2,1,0:T(8,128)(2,1)S(1)} %reshape.163), kind=kOutput, calls=%fused_computation.57 | convolution fusion | flops 17170464 | bytes 1589248 | tf_op jit(solution)/shard_map/sub | solution.py:44
  157.1 2.9 %fusion.18 = bf16[2,32,8,8,64]{4,1,3,2,0:T(8,128)(2,1)S(1)} fusion(f32[2,8,8,32,32]{3,4,2,1,0:T(8,128)} %get-tuple-element.14, bf16[2,32,8,8,64]{4,3,2,1,0:T(8,128)(2,1)} %reshape.162, f32[2,8,8,32]{3,2,1,0:T(8,128)S(1)} %get-tuple-element.13), kind=kOutput, calls=%fused_computation.31 | convolution fusion | flops 17301504 | bytes 1589248 | tf_op jit(solution)/shard_map/bmhlk,bkmhe->blmhe/dot_general | solution.py:46
  159.9 0.4 copy.99
  160.3 0.6 reshape.173
  161.0 37.9 %all_to_all.29 = bf16[2,32,8,512]{3,2,0,1:T(8,128)(2,1)S(1)} all-to-all(bf16[2,32,8,512]{3,2,0,1:T(8,128)(2,1)S(1)} %reshape.173), channel_id=1, replica_groups=mesh['fsdp'=16,'tm'=32] {'tm'}, dimensions={1} | all-to-all | bytes 1048576 | tf_op jit(solution)/shard_map/all_to_all | solution.py:93
  198.8 1.1 broadcast_in_dim.5
  199.9 3.7 %all-to-all-start.3 = ((bf16[16,32,1024]{2,1,0:T(8,128)(2,1)}), bf16[16,32,1024]{2,1,0:T(8,128)(2,1)S(1)}, u32[]{:S(2)}, u32[]{:S(2)}) async-start(bf16[16,32,1024]{2,1,0:T(8,128)(2,1)} %broadcast_in_dim.5), calls=%async_computation.3 | async-start | bytes 2097152 | tf_op jit(solution)/shard_map/all_to_all | solution.py:20
  203.7 16.4 %all-to-all-done.3 = bf16[16,32,1024]{2,1,0:T(8,128)(2,1)S(1)} async-done(((bf16[16,32,1024]{2,1,0:T(8,128)(2,1)}), bf16[16,32,1024]{2,1,0:T(8,128)(2,1)S(1)}, u32[]{:S(2)}, u32[]{:S(2)}) %all-to-all-start.3) | async-done | bytes 1048608 | tf_op jit(solution)/shard_map/all_to_all | solution.py:20
  220.1 1.7 add_convert_fusion
  (28 shorter events, 1.2 us)
Async XLA Ops:
  6.5 9.0 %copy-start = (bf16[2,1,256,1024]{3,2,1,0:T(8,128)(2,1)S(1)}, bf16[2,1,256,1024]{3,2,1,0:T(8,128)(2,1)}, u32[]{:S(2)}) copy-start(bf16[2,1,256,1024]{3,2,1,0:T(8,128)(2,1)} %param.7) | copy-start | bytes 3145732
  6.5 50.5 %all-gather.3.cloned.1.call-start = ((), (), s32[]{:S(2)}) async-start(), calls=%async_computation.4 | async-start | bytes 3342336 | tf_op jit(solution)/shard_map/all_gather | solution.py:58
  9.2 47.8 %copy-start.4 = (f32[1024]{0:T(1024)S(1)}, f32[1024]{0:T(1024)}, u32[]{:S(2)}) copy-start(f32[1024]{0:T(1024)} %param.8) | copy-start | bytes 12292
  9.2 59.2 %all-to-all-start = ((bf16[16,32,1024]{2,1,0:T(8,128)(2,1)}), bf16[16,32,1024]{2,1,0:T(8,128)(2,1)}, u32[]{:S(2)}, u32[]{:S(2)}) async-start(bf16[16,32,1024]{2,1,0:T(8,128)(2,1)} %broadcast_in_dim.4), calls=%async_computation | async-start | bytes 2097152 | tf_op jit(solution)/shard_map/all_to_all | solution.py:20
  14.8 132.3 %all-gather.5.cloned.1.call-start = ((), (), s32[]{:S(2)}) async-start(), calls=%async_computation.5 | async-start | bytes 3342336 | tf_op jit(solution)/shard_map/all_gather | solution.py:58
  70.3 72.5 %copy-start.1 = (bf16[512,1024]{1,0:T(8,128)(2,1)}, bf16[512,1024]{1,0:T(8,128)(2,1)S(1)}, u32[]{:S(2)}) copy-start(bf16[512,1024]{1,0:T(8,128)(2,1)S(1)} %fusion.8) | copy-start | bytes 3145732
  145.6 1.5 copy-start.5
  159.9 38.9 %copy-start.3 = (bf16[32,1024]{1,0:T(8,128)(2,1)S(1)}, bf16[32,1024]{1,0:T(8,128)(2,1)}, u32[]{:S(2)}) copy-start(bf16[32,1024]{1,0:T(8,128)(2,1)} %param.13) | copy-start | bytes 196612
  198.8 21.2 %copy-start.2 = (bf16[512,1024]{1,0:T(8,128)(2,1)S(1)}, bf16[512,1024]{1,0:T(8,128)(2,1)}, u32[]{:S(2)}) copy-start(bf16[512,1024]{1,0:T(8,128)(2,1)} %copy-done.1) | copy-start | bytes 3145732
  199.9 20.1 %all-to-all-start.3 = ((bf16[16,32,1024]{2,1,0:T(8,128)(2,1)}), bf16[16,32,1024]{2,1,0:T(8,128)(2,1)S(1)}, u32[]{:S(2)}, u32[]{:S(2)}) async-start(bf16[16,32,1024]{2,1,0:T(8,128)(2,1)} %broadcast_in_dim.5), calls=%async_computation.3 | async-start | bytes 2097152 | tf_op jit(solution)/shard_map/all_to_all | solution.py:20
Sparse Core Ops, SparseCore 0:
  9.5 47.4 all-gather.2
  59.1 44.3 all-gather.4
where the time goes:
time: 229 us
  blocking collectives  109 us (48%)
  waiting for transfers between devices  58.6 us (26%)
  matrix products  23.6 us (10%)
  between operations  13.6 us (6%)
  local copies, waits for them, and re-layouts  9.84 us (4%)
  starting transfers between devices  9.3 us (4%)
  other arithmetic  4.31 us (2%)
    all_to_all x1, blocking collectives, shards(): lax.all_to_all(middle, 'tm', split_axis=2, concat_axis=1, tiled=True)  71.4 us
    all_gather x2, waiting for transfers between devices, project_inputs(): lax.all_gather(weight, 'fsdp', axis=0, tiled=True)  40.8 us
    all_to_all x1, blocking collectives, shards(): lax.all_to_all(context_t, 'tm', split_axis=1, concat_axis=2, tiled=True)  37.9 us
    all_to_all x2, waiting for transfers between devices, sent_to_all(): return lax.all_to_all(copies, axis, split_axis=0, concat_axis=0, tiled=True)  16.4 us
    all_to_all x2, starting transfers between devices, sent_to_all(): return lax.all_to_all(copies, axis, split_axis=0, concat_axis=0, tiled=True)  9.25 us
    dot_general x2, matrix products, add_rows(): return jnp.dot(normed, segment, preferred_element_type=jnp.float32)  7.8 us
    sub x2, matrix products, attention_core(): exponent = jnp.exp(scores - row_max)  6.63 us
    dot_general x2, matrix products, attention_core(): jnp.einsum('bmhlk,bkmhe->blmhe', weights, value_rows, preferred_element_t...  5.53 us
  transfers between devices with their start and end apart: 4, of which 2 were waited for; matrix products, arithmetic and copies ran while one was open for 9% of the time, Pallas kernels for 0%

commit v1 on v0

--- a/solution.py
+++ b/solution.py
@@ -55,7 +55,13 @@
         return jnp.dot(normed, segment, preferred_element_type=jnp.float32)
 
     initial = jnp.zeros((normed.shape[0], weight.shape[1]), jnp.float32)
-    return add_rows(initial, lax.all_gather(weight, "fsdp", axis=0, tiled=True), jnp.int32(0))
+
+    def _convert_cube(local, along_axis="fsdp"):
+        return jnp.concatenate(
+            lax.all_to_all(jnp.stack(lax.axis_size(along_axis) * [local]), along_axis, 0, 0), axis=0
+        )
+
+    return add_rows(initial, _convert_cube(weight), jnp.int32(0))
 
 
 def project_outputs(context, weight):

time: 229 us -> 277 us (1.21)
  waiting for transfers between devices: 58.6 us -> 94.7 us
  starting transfers between devices: 9.3 us -> 26.7 us
  between operations: 13.6 us -> 0.25 us
  local copies, waits for them, and re-layouts: 9.84 us -> 14.4 us
  blocking collectives: 109 us -> 112 us
    all_to_all x0 -> x2, waiting for transfers between devices: none -> 73.1 us  [_convert_cube(): lax.all_to_all(jnp.stack(lax.axis_size(along_axis) * [local]), along_axis...]
    all_gather x2 -> x0, waiting for transfers between devices: 40.8 us -> none  [project_inputs(): lax.all_gather(weight, 'fsdp', axis=0, tiled=True)]
    all_to_all x0 -> x2, starting transfers between devices: none -> 10.3 us  [_convert_cube(): lax.all_to_all(jnp.stack(lax.axis_size(along_axis) * [local]), along_axis...]
    all_to_all x2, starting transfers between devices: 9.25 us -> 16.4 us  [sent_to_all(): return lax.all_to_all(copies, axis, split_axis=0, concat_axis=0, tiled=True)]
    all_to_all x2, waiting for transfers between devices: 16.4 us -> 21.6 us  [sent_to_all(): return lax.all_to_all(copies, axis, split_axis=0, concat_axis=0, tiled=True)]
    another operation x0 -> x2, local copies, waits for them, and re-layouts: none -> 4.94 us  [_convert_cube(): jnp.stack(lax.axis_size(along_axis) * [local])]
  transfers between devices with their start and end apart: 4 -> 4, of which waited for: 2 -> 4; matrix products, arithmetic and copies ran while one was open for 9% -> 6% of each run, Pallas kernels for 0% -> 0%
where the time goes in v1:
time: 277 us; the launch traced here: 276 us
  blocking collectives  112 us (40%)
  waiting for transfers between devices  94.7 us (34%)
  starting transfers between devices  26.7 us (10%)
  matrix products  23.3 us (8%)
  local copies, waits for them, and re-layouts  14.4 us (5%)
  other arithmetic  4.94 us (2%)
    all_to_all x1, blocking collectives, shards(): lax.all_to_all(middle, 'tm', split_axis=2, concat_axis=1, tiled=True)  73.4 us
    all_to_all x2, waiting for transfers between devices, _convert_cube(): lax.all_to_all(jnp.stack(lax.axis_size(along_axis) * [local]), along_axis...  73.1 us
    all_to_all x1, blocking collectives, shards(): lax.all_to_all(context_t, 'tm', split_axis=1, concat_axis=2, tiled=True)  38.4 us
    all_to_all x2, waiting for transfers between devices, sent_to_all(): return lax.all_to_all(copies, axis, split_axis=0, concat_axis=0, tiled=True)  21.6 us
    all_to_all x2, starting transfers between devices, sent_to_all(): return lax.all_to_all(copies, axis, split_axis=0, concat_axis=0, tiled=True)  16.4 us
    all_to_all x2, starting transfers between devices, _convert_cube(): lax.all_to_all(jnp.stack(lax.axis_size(along_axis) * [local]), along_axis...  10.3 us
    dot_general x2, matrix products, add_rows(): return jnp.dot(normed, segment, preferred_element_type=jnp.float32)  7.47 us
    sub x2, matrix products, attention_core(): exponent = jnp.exp(scores - row_max)  6.62 us
  transfers between devices with their start and end apart: 4, of which 4 were waited for; matrix products, arithmetic and copies ran while one was open for 6% of the time, Pallas kernels for 0%

profile of v1, /device:TPU:32, one launch (start us, length us, event | category | flops | bytes accessed | tf_op | source)
XLA Modules:
  0.0 276.1 jit_solution(40159349619842399)
XLA Ops:
  0.0 2.9 %stack.4 = bf16[16,64,1536]{2,1,0:T(8,128)(2,1)} broadcast(bf16[64,1536]{1,0:T(8,128)(2,1)} %param.9), dimensions={1,2} | broadcast | bytes 3342336 | tf_op jit(solution)/shard_map/stack | solution.py:61
  2.9 5.6 %all-to-all-start = ((bf16[16,64,1536]{2,1,0:T(8,128)(2,1)}), bf16[16,64,1536]{2,1,0:T(8,128)(2,1)}, u32[]{:S(2)}, u32[]{:S(2)}) async-start(bf16[16,64,1536]{2,1,0:T(8,128)(2,1)} %stack.4), calls=%async_computation | async-start | bytes 6291456 | tf_op jit(solution)/shard_map/all_to_all | solution.py:61
  9.2 38.5 %all-to-all-done = bf16[16,64,1536]{2,1,0:T(8,128)(2,1)} async-done(((bf16[16,64,1536]{2,1,0:T(8,128)(2,1)}), bf16[16,64,1536]{2,1,0:T(8,128)(2,1)}, u32[]{:S(2)}, u32[]{:S(2)}) %all-to-all-start) | async-done | bytes 3145760 | tf_op jit(solution)/shard_map/all_to_all | solution.py:61
  47.7 1.1 broadcast_in_dim.4
  48.8 8.6 %all-to-all-start.1 = ((bf16[16,32,1024]{2,1,0:T(8,128)(2,1)}), bf16[16,32,1024]{2,1,0:T(8,128)(2,1)}, u32[]{:S(2)}, u32[]{:S(2)}) async-start(bf16[16,32,1024]{2,1,0:T(8,128)(2,1)} %broadcast_in_dim.4), calls=%async_computation.1 | async-start | bytes 2097152 | tf_op jit(solution)/shard_map/all_to_all | solution.py:20
  57.5 3.8 %convolution_bitcast_fusion = bf16[2,256,1,1536]{3,1,0,2:T(8,128)(2,1)S(1)} fusion(bf16[1024,1536,1]{1,0,2:T(8,128)(2,1)} %bitcast.3, bf16[2,1,256,1024]{3,2,1,0:T(8,128)(2,1)S(1)} %copy-done, f32[1024]{0:T(1024)S(1)} %copy-done.7, f32[2,256]{1,0:T(2,128)S(1)} %add_rsqrt_fusion.1, f32[2,256]{1,0:T(2,128)S(1)} %broadcast_multiply_fusion.1), kind=kOutput, calls=%fused_computation.6 | convolution fusion | flops 1613234176 | bytes 5775360 | tf_op jit(solution)/shard_map/dot_general | solution.py:55
  62.0 3.4 %fusion.36 = (f32[2,8,256]{2,1,0:T(8,128)S(1)}, f32[2,8,256,256]{2,3,1,0:T(8,128)}) fusion(bf16[2,256,8,64]{1,3,2,0:T(8,128)(2,1)S(1)} %bitcast.67, bf16[2,256,8,64]{1,3,2,0:T(8,128)(2,1)S(1)} %bitcast.68), kind=kOutput, calls=%fused_computation.53 | convolution fusion | flops 137363712 | bytes 5259264 | tf_op jit(solution)/shard_map/sub | solution.py:44
  65.5 2.7 fusion.19
  68.2 0.5 copy.82
  68.8 5.2 %all-to-all-done.1 = bf16[16,32,1024]{2,1,0:T(8,128)(2,1)} async-done(((bf16[16,32,1024]{2,1,0:T(8,128)(2,1)}), bf16[16,32,1024]{2,1,0:T(8,128)(2,1)}, u32[]{:S(2)}, u32[]{:S(2)}) %all-to-all-start.1) | async-done | bytes 1048608 | tf_op jit(solution)/shard_map/all_to_all | solution.py:20
  74.0 2.0 fusion.10
  75.9 1.0 copy-done.1
  76.9 1.1 copy.83
  78.0 73.4 %all_to_all.38 = bf16[2,1,256,1024]{3,0,1,2:T(2,128)(2,1)S(1)} all-to-all(bf16[2,1,256,1024]{3,0,1,2:T(2,128)(2,1)S(1)} %copy.83), channel_id=1, replica_groups=mesh['fsdp'=16,'tm'=32] {'tm'}, dimensions={2} | all-to-all | bytes 2097152 | tf_op jit(solution)/shard_map/all_to_all | solution.py:91
  151.4 2.0 stack.5
  153.5 4.7 %all-to-all-start.3 = ((bf16[16,64,1536]{2,1,0:T(8,128)(2,1)}), bf16[16,64,1536]{2,1,0:T(8,128)(2,1)}, u32[]{:S(2)}, u32[]{:S(2)}) async-start(bf16[16,64,1536]{2,1,0:T(8,128)(2,1)} %stack.5), calls=%async_computation.3 | async-start | bytes 6291456 | tf_op jit(solution)/shard_map/all_to_all | solution.py:61
  158.1 0.9 convert_reduce_fusion
  159.0 1.8 fusion.7
  160.9 1.6 fusion.9
  162.5 34.6 %all-to-all-done.3 = bf16[16,64,1536]{2,1,0:T(8,128)(2,1)} async-done(((bf16[16,64,1536]{2,1,0:T(8,128)(2,1)}), bf16[16,64,1536]{2,1,0:T(8,128)(2,1)}, u32[]{:S(2)}, u32[]{:S(2)}) %all-to-all-start.3) | async-done | bytes 3145760 | tf_op jit(solution)/shard_map/all_to_all | solution.py:61
  197.1 3.7 %fusion.23 = bf16[2,32,8,1536]{3,2,1,0:T(8,128)(2,1)S(1)} fusion(bf16[1024,1536,1,1]{1,0,3,2:T(8,128)(2,1)} %bitcast.15, bf16[2,32,8,1024]{3,0,2,1:T(2,128)(2,1)S(1)} %bitcast.63), kind=kOutput, calls=%fused_computation.37 | convolution fusion | flops 1610612736 | bytes 5767168 | tf_op jit(solution)/shard_map/dot_general | solution.py:55
  200.9 0.5 reshape.180
  201.5 0.5 reshape.179
  202.0 1.5 reshape.178
  203.5 3.2 %fusion.37 = (f32[2,8,8,32]{3,2,1,0:T(8,128)S(1)}, f32[2,8,8,32,32]{3,4,2,1,0:T(8,128)}) fusion(bf16[2,32,8,8,64]{4,3,2,1,0:T(8,128)(2,1)S(1)} %reshape.180, bf16[2,32,8,8,64]{4,3,2,1,0:T(8,128)(2,1)S(1)} %reshape.179), kind=kOutput, calls=%fused_computation.54 | convolution fusion | flops 17170464 | bytes 1589248 | tf_op jit(solution)/shard_map/sub | solution.py:44
  206.7 2.9 %fusion.17 = bf16[2,32,8,8,64]{4,1,3,2,0:T(8,128)(2,1)S(1)} fusion(f32[2,8,8,32,32]{3,4,2,1,0:T(8,128)} %get-tuple-element.14, bf16[2,32,8,8,64]{4,3,2,1,0:T(8,128)(2,1)} %reshape.178, f32[2,8,8,32]{3,2,1,0:T(8,128)S(1)} %get-tuple-element.13), kind=kOutput, calls=%fused_computation.30 | convolution fusion | flops 17301504 | bytes 1589248 | tf_op jit(solution)/shard_map/bmhlk,bkmhe->blmhe/dot_general | solution.py:46
  210.0 0.6 reshape.188
  210.6 38.4 %all_to_all.39 = bf16[2,32,8,512]{3,2,0,1:T(8,128)(2,1)S(1)} all-to-all(bf16[2,32,8,512]{3,2,0,1:T(8,128)(2,1)S(1)} %reshape.188), channel_id=1, replica_groups=mesh['fsdp'=16,'tm'=32] {'tm'}, dimensions={1} | all-to-all | bytes 1048576 | tf_op jit(solution)/shard_map/all_to_all | solution.py:99
  249.0 1.1 broadcast_in_dim.5
  250.1 7.8 %all-to-all-start.5 = ((bf16[16,32,1024]{2,1,0:T(8,128)(2,1)}), bf16[16,32,1024]{2,1,0:T(8,128)(2,1)S(1)}, u32[]{:S(2)}, u32[]{:S(2)}) async-start(bf16[16,32,1024]{2,1,0:T(8,128)(2,1)} %broadcast_in_dim.5), calls=%async_computation.5 | async-start | bytes 2097152 | tf_op jit(solution)/shard_map/all_to_all | solution.py:20
  258.0 16.4 %all-to-all-done.5 = bf16[16,32,1024]{2,1,0:T(8,128)(2,1)S(1)} async-done(((bf16[16,32,1024]{2,1,0:T(8,128)(2,1)}), bf16[16,32,1024]{2,1,0:T(8,128)(2,1)S(1)}, u32[]{:S(2)}, u32[]{:S(2)}) %all-to-all-start.5) | async-done | bytes 1048608 | tf_op jit(solution)/shard_map/all_to_all | solution.py:20
  274.4 1.7 add_convert_fusion
  (29 shorter events, 2.1 us)
Async XLA Ops:
  2.9 5.6 %copy-start = (bf16[2,1,256,1024]{3,2,1,0:T(8,128)(2,1)S(1)}, bf16[2,1,256,1024]{3,2,1,0:T(8,128)(2,1)}, u32[]{:S(2)}) copy-start(bf16[2,1,256,1024]{3,2,1,0:T(8,128)(2,1)} %param.7) | copy-start | bytes 3145732
  2.9 44.8 %all-to-all-start = ((bf16[16,64,1536]{2,1,0:T(8,128)(2,1)}), bf16[16,64,1536]{2,1,0:T(8,128)(2,1)}, u32[]{:S(2)}, u32[]{:S(2)}) async-start(bf16[16,64,1536]{2,1,0:T(8,128)(2,1)} %stack.4), calls=%async_computation | async-start | bytes 6291456 | tf_op jit(solution)/shard_map/all_to_all | solution.py:61
  8.5 39.2 %copy-start.4 = (bf16[32,1024]{1,0:T(8,128)(2,1)S(1)}, bf16[32,1024]{1,0:T(8,128)(2,1)}, u32[]{:S(2)}) copy-start(bf16[32,1024]{1,0:T(8,128)(2,1)} %param.10) | copy-start | bytes 196612
  8.8 48.7 %copy-start.7 = (f32[1024]{0:T(1024)S(1)}, f32[1024]{0:T(1024)}, u32[]{:S(2)}) copy-start(f32[1024]{0:T(1024)} %param.8) | copy-start | bytes 12292
  48.8 25.2 %all-to-all-start.1 = ((bf16[16,32,1024]{2,1,0:T(8,128)(2,1)}), bf16[16,32,1024]{2,1,0:T(8,128)(2,1)}, u32[]{:S(2)}, u32[]{:S(2)}) async-start(bf16[16,32,1024]{2,1,0:T(8,128)(2,1)} %broadcast_in_dim.4), calls=%async_computation.1 | async-start | bytes 2097152 | tf_op jit(solution)/shard_map/all_to_all | solution.py:20
  75.9 1.0 copy-start.1
  76.9 74.5 %copy-start.3 = (bf16[64,1536]{1,0:T(8,128)(2,1)S(1)}, bf16[64,1536]{1,0:T(8,128)(2,1)}, u32[]{:S(2)}) copy-start(bf16[64,1536]{1,0:T(8,128)(2,1)} %param.12) | copy-start | bytes 589828
  153.5 43.6 %all-to-all-start.3 = ((bf16[16,64,1536]{2,1,0:T(8,128)(2,1)}), bf16[16,64,1536]{2,1,0:T(8,128)(2,1)}, u32[]{:S(2)}, u32[]{:S(2)}) async-start(bf16[16,64,1536]{2,1,0:T(8,128)(2,1)} %stack.5), calls=%async_computation.3 | async-start | bytes 6291456 | tf_op jit(solution)/shard_map/all_to_all | solution.py:61
  158.1 2.8 %copy-start.6 = (f32[1024]{0:T(1024)S(1)}, f32[1024]{0:T(1024)}, u32[]{:S(2)}) copy-start(f32[1024]{0:T(1024)} %param.11) | copy-start | bytes 12292
  209.6 39.4 %copy-start.5 = (bf16[32,1024]{1,0:T(8,128)(2,1)S(1)}, bf16[32,1024]{1,0:T(8,128)(2,1)}, u32[]{:S(2)}) copy-start(bf16[32,1024]{1,0:T(8,128)(2,1)} %param.13) | copy-start | bytes 196612
  249.0 25.4 %copy-start.2 = (bf16[512,1024]{1,0:T(8,128)(2,1)S(1)}, bf16[512,1024]{1,0:T(8,128)(2,1)}, u32[]{:S(2)}) copy-start(bf16[512,1024]{1,0:T(8,128)(2,1)} %copy-done.1) | copy-start | bytes 3145732
  250.1 24.3 %all-to-all-start.5 = ((bf16[16,32,1024]{2,1,0:T(8,128)(2,1)}), bf16[16,32,1024]{2,1,0:T(8,128)(2,1)S(1)}, u32[]{:S(2)}, u32[]{:S(2)}) async-start(bf16[16,32,1024]{2,1,0:T(8,128)(2,1)} %broadcast_in_dim.5), calls=%async_computation.5 | async-start | bytes 2097152 | tf_op jit(solution)/shard_map/all_to_all | solution.py:20
